TPU v7x, 32 devices: a whole 2x2x4 slice. The times are simulated.
32 devices in a mesh: pp: 2 (over core), cp: 4 (over y, x), tp: 4 (over z).
Axes of the slice: x: 2, y: 2, z: 4, core: 2. Of those that a mesh axis runs over, the one named last changes fastest.
Arguments:
- query: bfloat16 [2, 512, 4096], P('pp', 'cp', 'tp'), may hold values from -120 to 120
- keyval: bfloat16 [2, 2, 512, 1024], P('pp', None, 'cp', 'tp'), may hold values from -4 to 4
- out_weight: bfloat16 [2, 4096, 4096], P('pp', None, 'tp'), may hold values from -0.375 to 0.375
- residual: bfloat16 [2, 512, 4096], P('pp', 'cp', 'tp'), may hold values from -3 to 3
- block_order: int32 [8], replicated, may hold values from 0 to 7, as said below
Outputs:
- handed: bfloat16 [2, 512, 4096], P('pp', 'cp', 'tp')
Inputs may be any that keep to these rules, and one draw needn't show every extreme that they name: A permutation of the 8 sequence blocks; context index c holds blocks block_order[2 c] and block_order[2 c + 1] in its first and second 64 rows.
All inputs are finite; a program needn't handle non-finite values.
Results may differ from a plain program's by a relative error of at most 0.013.
Values may be sent and summed in bfloat16 or wider, within the bound.
No kernel may reach another device: no remote copies, remote signals or barrier semaphores. Data moves between devices by JAX's collectives and lax.ppermute only.
A program may use at most 64 MiB of HBM per device.

v0:
```python
import math
import jax
import jax.numpy as jnp
from jax import lax
from jax.sharding import PartitionSpec as P

HD = 128
GROUP = 4
LOW_SCORE = -1e30


def shifted(value, axis, steps):
    count = lax.axis_size(axis)
    pairs = [(source, (source + steps) % count) for source in range(count)]
    return lax.ppermute(value, axis, pairs)


def positions(row_index, block_order, shard_rows, half_rows):
    slot_index = 2 * (row_index // shard_rows) + row_index % shard_rows // half_rows
    lookup = jnp.arange(block_order.shape[0], dtype=jnp.int32)
    picked = jnp.sum(
        jnp.where(slot_index[:, None] == lookup[None, :], block_order[None, :], 0), axis=1
    )
    return picked * half_rows + row_index % half_rows


def attend_piece(carried, queries, query_pos, key_rows, values, key_pos):
    weighted, row_peak, row_mass = carried
    scores = jnp.einsum("qkgd,nkd->qkgn", queries, key_rows, preferred_element_type=jnp.float32) * (
        1.0 / math.sqrt(HD)
    )
    visible = (key_pos[None, :] <= query_pos[:, None])[:, None, None, :]
    scores = jnp.where(visible, scores, LOW_SCORE)
    new_peak = jnp.maximum(row_peak, jnp.max(scores, axis=3))
    factor = jnp.exp(row_peak - new_peak)
    weights = jnp.where(visible, jnp.exp(scores - new_peak[..., None]), 0.0)
    rounded = weights.astype(jnp.bfloat16)
    weighted = weighted * factor[..., None] + jnp.einsum(
        "qkgn,nkd->qkgd", rounded, values, preferred_element_type=jnp.float32
    )
    row_mass = row_mass * factor + jnp.sum(weights, axis=3)
    return (weighted, new_peak, row_mass)


def guarded(carried, queries, query_pos, key_rows, values, key_pos):
    return attend_piece(carried, queries, query_pos, key_rows, values, key_pos)


def fold_rows(carried, queries, query_pos, key_rows, values, key_pos):
    total = key_rows.shape[0]
    if total <= 512 or total % 512 != 0:
        return guarded(carried, queries, query_pos, key_rows, values, key_pos)
    count = total // 512
    stacked = (
        key_rows.reshape((count, 512) + key_rows.shape[1:]),
        values.reshape((count, 512) + values.shape[1:]),
        key_pos.reshape(count, 512),
    )

    def advance(inner, block_in):
        return (guarded(inner, queries, query_pos, block_in[0], block_in[1], block_in[2]), None)

    result, unused = lax.scan(advance, carried, stacked)
    return result


def start_state(shard_rows, kv_count):
    return (
        jnp.zeros((shard_rows, kv_count, GROUP, HD), jnp.float32),
        jnp.full((shard_rows, kv_count, GROUP), LOW_SCORE, jnp.float32),
        jnp.zeros((shard_rows, kv_count, GROUP), jnp.float32),
    )


def local(query, keyval, out_weight, residual, block_order):
    shard_rows = query.shape[1]
    half_rows = shard_rows // 2
    cp_index = lax.axis_index("cp")
    own_rows = cp_index * shard_rows + jnp.arange(shard_rows, dtype=jnp.int32)
    query_pos = positions(own_rows, block_order, shard_rows, half_rows)
    weight = out_weight[0]
    kv_count = keyval.shape[3] // HD
    queries = query[0].reshape(shard_rows, kv_count, GROUP, HD)
    block_in = lax.all_gather(keyval, "cp", axis=2, tiled=True)
    piece_rows = block_in.shape[2]
    row_index = jnp.arange(piece_rows, dtype=jnp.int32)
    key_pos = positions(row_index, block_order, shard_rows, half_rows)
    key_rows = block_in[0, 0].reshape(piece_rows, kv_count, HD)
    values = block_in[0, 1].reshape(piece_rows, kv_count, HD)
    weighted, row_peak, row_mass = fold_rows(
        start_state(shard_rows, kv_count), queries, query_pos, key_rows, values, key_pos
    )
    own_heads = (
        (weighted / row_mass[..., None])
        .reshape(shard_rows, kv_count * GROUP * HD)
        .astype(jnp.bfloat16)
    )
    attended = lax.all_gather(own_heads, "tp", axis=1, tiled=True)
    resid_rows = residual[0]
    mixed_sum = jnp.dot(attended, weight, preferred_element_type=jnp.float32)
    layer_out = (mixed_sum + resid_rows.astype(jnp.float32)).astype(jnp.bfloat16)[None]
    return shifted(layer_out, "pp", 1)


def solution(mesh):
    placed = (
        P("pp", "cp", "tp"),
        P("pp", None, "cp", "tp"),
        P("pp", None, "tp"),
        P("pp", "cp", "tp"),
        P(),
    )
    return jax.shard_map(
        local, mesh=mesh, in_specs=placed, out_specs=P("pp", "cp", "tp"), check_vma=False
    )
```

profile of v0, /device:TPU:0, one launch (start us, length us, event | category | flops | bytes accessed | tf_op | source)
XLA Modules:
  0.0 67.0 jit_solution(8327772678584267992)
XLA Ops:
  6.5 0.0 all-gather.2.cloned.1.call-start
  6.6 0.7 %select_reduce_fusion.1 = s32[128]{0:T(128)S(1)} fusion(s32[8]{0:T(128)} %param.9, s32[128]{0:T(128)S(1)} %fusion.40), kind=kLoop, calls=%fused_computation.24 | loop fusion | flops 2944 | bytes 1056 | tf_op jit(solution)/shard_map/reduce_sum | solution.py:21
  7.3 0.7 %select_reduce_fusion = s32[512]{0:T(512)S(1)} fusion(s32[8]{0:T(128)} %param.9, s32[512]{0:T(512)S(1)} %fusion.29), kind=kLoop, calls=%fused_computation.21 | loop fusion | flops 11776 | bytes 4128 | tf_op jit(solution)/shard_map/reduce_sum | solution.py:21
  8.1 1.0 %copy.13 = bf16[1,2,128,256]{2,3,1,0:T(8,128)(2,1)S(1)} copy(bf16[1,2,128,256]{3,2,1,0:T(8,128)(2,1)} %param.6) | data formatting | bytes 262144 | tf_op args[1]
  9.1 1.1 %reshape_squeeze.10 = bf16[128,2,4,128]{3,2,1,0:T(4,128)(2,1)S(1)} reshape(bf16[1,128,1024]{2,1,0:T(8,128)(2,1)} %param.5) | data formatting | bytes 524288 | tf_op jit(solution)/shard_map/reshape;squeeze | solution.py:83
  10.2 11.5 %all_gather.6 = bf16[1,2,512,256]{2,3,1,0:T(8,128)(2,1)S(1)} all-gather(bf16[1,2,128,256]{2,3,1,0:T(8,128)(2,1)S(1)} %copy.13), channel_id=1, replica_groups=mesh['pp'=2,'cp'=4,'tp'=4] {'cp'}, dimensions={2}, use_global_device_ids=true | all-gather | bytes 655360 | tf_op jit(solution)/shard_map/all_gather | solution.py:84
  21.8 0.1 broadcast_compare_fusion
  21.9 0.5 fusion.2
  22.5 0.5 fusion.3
  23.0 0.0 copy-start
  23.0 1.4 %fusion.13 = bf16[128,2,4,128]{0,3,2,1:T(8,128)(2,1)} fusion(bf16[512,2,128,1]{0,2,3,1:T(8,128)(2,1)S(1)} %bitcast.49, f32[2,512,128,4]{2,1,3,0:T(8,128)S(1)} %get-tuple-element.10, f32[128,2,4]{0,2,1:T(4,128)S(1)} %broadcast_maximum_fusion, pred[128,512]{0,1:T(8,128)(4,1)S(1)} %broadcast_compare_fusion, f32[128,2,4]{0,2,1:T(4,128)S(1)} %get-tuple-element.8, ...), kind=kOutput, calls=%fused_computation.12 | convolution fusion | flops 137232384 | bytes 2699264 | tf_op jit(solution)/shard_map/qkgn,nkd->qkgd/dot_general | solution.py:38
  24.4 0.0 all-gather.2.cloned.1.call-update
  24.4 28.4 %all-gather.2.cloned.1.call-done = bf16[128,4096]{0,1:T(8,128)(2,1)} async-done(((bf16[128,1024]{0,1:T(8,128)(2,1)}), bf16[128,4096]{0,1:T(8,128)(2,1)}) %all-gather.2.cloned.1.call-update) | async-done | bytes 1048592 | tf_op jit(solution)/shard_map/all_gather | solution.py:98
  52.9 0.0 copy-done
  52.9 5.0 %fusion.14 = bf16[1,128,1024]{2,1,0:T(8,128)(2,1)S(1)} fusion(bf16[128,4096]{0,1:T(8,128)(2,1)} %all-gather.2.cloned.1.call-done, bf16[1,4096,1024]{2,1,0:T(8,128)(2,1)} %param.7, bf16[1,128,1024]{2,1,0:T(8,128)(2,1)S(1)} %copy-done), kind=kOutput, calls=%fused_computation.13 | convolution fusion | flops 1074135040 | bytes 9961472 | tf_op jit(solution)/shard_map/dot_general | solution.py:100
  57.9 0.1 collective-permute-start
  57.9 1.5 %collective-permute-done = bf16[1,128,1024]{2,1,0:T(8,128)(2,1)S(1)} collective-permute-done((bf16[1,128,1024]{2,1,0:T(8,128)(2,1)S(1)}, bf16[1,128,1024]{2,1,0:T(8,128)(2,1)S(1)}, u32[]{:S(2)}, u32[]{:S(2)}) %collective-permute-start) | collective-permute-done | bytes 262176 | tf_op jit(solution)/shard_map/ppermute | solution.py:15
  59.5 0.7 %copy.27 = bf16[1,128,1024]{2,1,0:T(8,128)(2,1)} copy(bf16[1,128,1024]{2,1,0:T(8,128)(2,1)S(1)} %collective-permute-done) | data formatting | bytes 524288
  (7 shorter events, 0.1 us)
Async XLA Ops:
  6.5 46.3 %all-gather.2.cloned.1.call-start = ((), (), s32[]{:S(2)}) async-start(), calls=%async_computation | async-start | bytes 1310720 | tf_op jit(solution)/shard_map/all_gather | solution.py:98
  23.0 29.8 %copy-start = (bf16[1,128,1024]{2,1,0:T(8,128)(2,1)S(1)}, bf16[1,128,1024]{2,1,0:T(8,128)(2,1)}, u32[]{:S(2)}) copy-start(bf16[1,128,1024]{2,1,0:T(8,128)(2,1)} %param.8) | copy-start | bytes 786436
  57.9 1.6 %collective-permute-start = (bf16[1,128,1024]{2,1,0:T(8,128)(2,1)S(1)}, bf16[1,128,1024]{2,1,0:T(8,128)(2,1)S(1)}, u32[]{:S(2)}, u32[]{:S(2)}) collective-permute-start(bf16[1,128,1024]{2,1,0:T(8,128)(2,1)S(1)} %fusion.14), channel_id=1, source_target_pairs={{0,16},{16,0},{1,17},{17,1},{2,18},{18,2},{3,19},{19,3},{4,20},{20... | collective-permute-start | bytes 786440 | tf_op jit(solution)/shard_map/ppermute | solution.py:15
Sparse Core Ops, SparseCore 0:
  24.6 28.2 all-gather.1
where the time goes:
time: 67.2 us; the launch traced here: 67 us
  waiting for transfers between devices  30 us (45%)
  between operations  13.5 us (20%)
  blocking collectives  11.5 us (17%)
  matrix products  6.91 us (10%)
  local copies, waits for them, and re-layouts  2.88 us (4%)
  other arithmetic  2.2 us (3%)
    all_gather x1, waiting for transfers between devices, local(): attended = lax.all_gather(own_heads, 'tp', axis=1, tiled=True)  28.4 us
    all_gather x1, blocking collectives, local(): block_in = lax.all_gather(keyval, 'cp', axis=2, tiled=True)  11.5 us
    dot_general x1, matrix products, local(): mixed_sum = jnp.dot(attended, weight, preferred_element_type=jnp.float32)  4.99 us
    unnamed x4, local copies, waits for them, and re-layouts  1.73 us
    ppermute x1, waiting for transfers between devices, shifted(): return lax.ppermute(value, axis, pairs)  1.52 us
    reduce_sum x2, other arithmetic, positions(): jnp.sum(jnp.where(slot_index[:, None] == lookup[None, :], block_order[Non...  1.48 us
    dot_general x1, matrix products, attend_piece(): jnp.einsum('qkgn,nkd->qkgd', rounded, values, preferred_element_type=jnp....  1.37 us
  transfers between devices with their start and end apart: 2, of which 2 were waited for; matrix products, arithmetic and copies ran while one was open for 0% of the time, Pallas kernels for 0%

commit v1 on v0

--- a/solution.py
+++ b/solution.py
@@ -81,7 +81,12 @@
     weight = out_weight[0]
     kv_count = keyval.shape[3] // HD
     queries = query[0].reshape(shard_rows, kv_count, GROUP, HD)
-    block_in = lax.all_gather(keyval, "cp", axis=2, tiled=True)
+    ring = [keyval]
+    for hop in range(3):
+        ring.append(lax.ppermute(ring[-1], "cp", [(dev, (dev + 1) % 4) for dev in range(4)]))
+    block_in = jnp.roll(
+        jnp.concatenate(ring[::-1], axis=2), (lax.axis_index("cp") + 1) * ring[0].shape[2], axis=2
+    )
     piece_rows = block_in.shape[2]
     row_index = jnp.arange(piece_rows, dtype=jnp.int32)
     key_pos = positions(row_index, block_order, shard_rows, half_rows)

time: 67.2 us -> 72.7 us (1.082)
  waiting for transfers between devices: 30 us -> 42.8 us
  blocking collectives: 11.5 us -> 0 us
  starting transfers between devices: 0.07 us -> 3.88 us
    ppermute x0 -> x3, waiting for transfers between devices: none -> 12.6 us  [local(): lax.ppermute(ring[-1], 'cp', [(dev, (dev + 1) % 4) for dev in range(4)])]
    all_gather x1 -> x0, blocking collectives: 11.5 us -> none  [local(): block_in = lax.all_gather(keyval, 'cp', axis=2, tiled=True)]
    ppermute x0 -> x3, starting transfers between devices: none -> 3.81 us  [local(): lax.ppermute(ring[-1], 'cp', [(dev, (dev + 1) % 4) for dev in range(4)])]
    unnamed x4 -> x11, local copies, waits for them, and re-layouts: 1.73 us -> 1.99 us
  transfers between devices with their start and end apart: 2 -> 5, of which waited for: 2 -> 5; matrix products, arithmetic and copies ran while one was open for 0% -> 4% of each run, Pallas kernels for 0% -> 0%
where the time goes in v1:
time: 72.7 us; the launch traced here: 72.5 us
  waiting for transfers between devices  42.8 us (59%)
  between operations  13.5 us (19%)
  matrix products  6.92 us (10%)
  starting transfers between devices  3.88 us (5%)
  local copies, waits for them, and re-layouts  3.2 us (4%)
  other arithmetic  2.2 us (3%)
    all_gather x1, waiting for transfers between devices, local(): attended = lax.all_gather(own_heads, 'tp', axis=1, tiled=True)  28.7 us
    ppermute x3, waiting for transfers between devices, local(): lax.ppermute(ring[-1], 'cp', [(dev, (dev + 1) % 4) for dev in range(4)])  12.6 us
    dot_general x1, matrix products, local(): mixed_sum = jnp.dot(attended, weight, preferred_element_type=jnp.float32)  5 us
    ppermute x3, starting transfers between devices, local(): lax.ppermute(ring[-1], 'cp', [(dev, (dev + 1) % 4) for dev in range(4)])  3.81 us
    unnamed x11, local copies, waits for them, and re-layouts  1.99 us
    ppermute x1, waiting for transfers between devices, shifted(): return lax.ppermute(value, axis, pairs)  1.52 us
    reduce_sum x2, other arithmetic, positions(): jnp.sum(jnp.where(slot_index[:, None] == lookup[None, :], block_order[Non...  1.48 us
  transfers between devices with their start and end apart: 5, of which 5 were waited for; matrix products, arithmetic and copies ran while one was open for 4% of the time, Pallas kernels for 0%

profile of v1, /device:TPU:0, one launch (start us, length us, event | category | flops | bytes accessed | tf_op | source)
XLA Modules:
  0.0 72.5 jit_solution(2058970213779241515)
XLA Ops:
  6.5 0.0 all-gather.2.cloned.1.call-start
  6.5 1.0 %copy.15 = bf16[1,2,128,256]{2,3,1,0:T(8,128)(2,1)S(1)} copy(bf16[1,2,128,256]{3,2,1,0:T(8,128)(2,1)} %param.6) | data formatting | bytes 262144 | tf_op args[1]
  7.6 3.0 %collective-permute-start = (bf16[1,2,128,256]{2,3,1,0:T(8,128)(2,1)S(1)}, bf16[1,2,128,256]{2,3,1,0:T(8,128)(2,1)S(1)}, u32[]{:S(2)}, u32[]{:S(2)}) collective-permute-start(bf16[1,2,128,256]{2,3,1,0:T(8,128)(2,1)S(1)} %copy.15), channel_id=1, source_target_pairs={{0,4},{4,8},{8,12},{12,0},{1,5},{5,9},{9,13},{13,1},{2,6},{6,10},{... | collective-permute-start | bytes 393224 | tf_op jit(solution)/shard_map/ppermute | solution.py:86
  10.6 0.7 %select_reduce_fusion = s32[512]{0:T(512)S(1)} fusion(s32[8]{0:T(128)} %param.9, s32[512]{0:T(512)S(1)} %fusion.29), kind=kLoop, calls=%fused_computation.29 | loop fusion | flops 11776 | bytes 4128 | tf_op jit(solution)/shard_map/reduce_sum | solution.py:21
  11.4 1.1 %reshape_squeeze.10 = bf16[128,2,4,128]{3,2,1,0:T(4,128)(2,1)S(1)} reshape(bf16[1,128,1024]{2,1,0:T(8,128)(2,1)} %param.5) | data formatting | bytes 524288 | tf_op jit(solution)/shard_map/reshape;squeeze | solution.py:83
  12.5 0.7 %select_reduce_fusion.1 = s32[128]{0:T(128)S(1)} fusion(s32[8]{0:T(128)} %param.9, s32[128]{0:T(128)S(1)} %fusion.40), kind=kLoop, calls=%fused_computation.32 | loop fusion | flops 2944 | bytes 1056 | tf_op jit(solution)/shard_map/reduce_sum | solution.py:21
  13.2 1.8 %collective-permute-done = bf16[1,2,128,256]{2,3,1,0:T(8,128)(2,1)S(1)} collective-permute-done((bf16[1,2,128,256]{2,3,1,0:T(8,128)(2,1)S(1)}, bf16[1,2,128,256]{2,3,1,0:T(8,128)(2,1)S(1)}, u32[]{:S(2)}, u32[]{:S(2)}) %collective-permute-start) | collective-permute-done | bytes 131104 | tf_op jit(solution)/shard_map/ppermute | solution.py:86
  15.0 0.8 %collective-permute-start.1 = (bf16[1,2,128,256]{2,3,1,0:T(8,128)(2,1)S(1)}, bf16[1,2,128,256]{2,3,1,0:T(8,128)(2,1)S(1)}, u32[]{:S(2)}, u32[]{:S(2)}) collective-permute-start(bf16[1,2,128,256]{2,3,1,0:T(8,128)(2,1)S(1)} %collective-permute-done), channel_id=1, source_target_pairs={{0,4},{4,8},{8,12},{12,0},{1,5},{5,9},{9,13},{13,1},{2,6},{6,10},{... | collective-permute-start | bytes 393224 | tf_op jit(solution)/shard_map/ppermute | solution.py:86
  15.8 5.1 %collective-permute-done.1 = bf16[1,2,128,256]{2,3,1,0:T(8,128)(2,1)S(1)} collective-permute-done((bf16[1,2,128,256]{2,3,1,0:T(8,128)(2,1)S(1)}, bf16[1,2,128,256]{2,3,1,0:T(8,128)(2,1)S(1)}, u32[]{:S(2)}, u32[]{:S(2)}) %collective-permute-start.1) | collective-permute-done | bytes 131104 | tf_op jit(solution)/shard_map/ppermute | solution.py:86
  20.9 0.0 collective-permute-start.2
  20.9 0.1 broadcast_compare_fusion
  21.0 5.7 %collective-permute-done.2 = bf16[1,2,128,256]{2,3,1,0:T(8,128)(2,1)S(1)} collective-permute-done((bf16[1,2,128,256]{2,3,1,0:T(8,128)(2,1)S(1)}, bf16[1,2,128,256]{2,3,1,0:T(8,128)(2,1)S(1)}, u32[]{:S(2)}, u32[]{:S(2)}) %collective-permute-start.2) | collective-permute-done | bytes 131104 | tf_op jit(solution)/shard_map/ppermute | solution.py:86
  27.2 0.5 fusion.2
  27.7 0.5 fusion.3
  28.3 0.0 copy-start
  28.3 1.4 %fusion.13 = bf16[128,2,4,128]{0,3,2,1:T(8,128)(2,1)} fusion(bf16[512,2,128,1]{0,2,3,1:T(8,128)(2,1)S(1)} %bitcast.48, f32[2,512,128,4]{2,1,3,0:T(8,128)S(1)} %get-tuple-element.10, f32[128,2,4]{0,2,1:T(4,128)S(1)} %broadcast_maximum_fusion, pred[128,512]{0,1:T(8,128)(4,1)S(1)} %broadcast_compare_fusion, f32[128,2,4]{0,2,1:T(4,128)S(1)} %get-tuple-element.8, ...), kind=kOutput, calls=%fused_computation.12 | convolution fusion | flops 137232384 | bytes 2699264 | tf_op jit(solution)/shard_map/qkgn,nkd->qkgd/dot_general | solution.py:38
  29.7 0.0 all-gather.2.cloned.1.call-update
  29.7 28.7 %all-gather.2.cloned.1.call-done = bf16[128,4096]{0,1:T(8,128)(2,1)} async-done(((bf16[128,1024]{0,1:T(8,128)(2,1)}), bf16[128,4096]{0,1:T(8,128)(2,1)}) %all-gather.2.cloned.1.call-update) | async-done | bytes 1048592 | tf_op jit(solution)/shard_map/all_gather | solution.py:103
  58.3 0.0 copy-done
  58.3 5.0 %fusion.14 = bf16[1,128,1024]{2,1,0:T(8,128)(2,1)S(1)} fusion(bf16[128,4096]{0,1:T(8,128)(2,1)} %all-gather.2.cloned.1.call-done, bf16[1,4096,1024]{2,1,0:T(8,128)(2,1)} %param.7, bf16[1,128,1024]{2,1,0:T(8,128)(2,1)S(1)} %copy-done), kind=kOutput, calls=%fused_computation.13 | convolution fusion | flops 1074135040 | bytes 9961472 | tf_op jit(solution)/shard_map/dot_general | solution.py:105
  63.4 0.1 collective-permute-start.3
  63.4 1.5 %collective-permute-done.3 = bf16[1,128,1024]{2,1,0:T(8,128)(2,1)S(1)} collective-permute-done((bf16[1,128,1024]{2,1,0:T(8,128)(2,1)S(1)}, bf16[1,128,1024]{2,1,0:T(8,128)(2,1)S(1)}, u32[]{:S(2)}, u32[]{:S(2)}) %collective-permute-start.3) | collective-permute-done | bytes 262176 | tf_op jit(solution)/shard_map/ppermute | solution.py:15
  65.0 0.7 copy.38
  (15 shorter events, 0.4 us)
Async XLA Ops:
  6.5 51.8 %all-gather.2.cloned.1.call-start = ((), (), s32[]{:S(2)}) async-start(), calls=%async_computation | async-start | bytes 1310720 | tf_op jit(solution)/shard_map/all_gather | solution.py:103
  7.6 7.5 %collective-permute-start = (bf16[1,2,128,256]{2,3,1,0:T(8,128)(2,1)S(1)}, bf16[1,2,128,256]{2,3,1,0:T(8,128)(2,1)S(1)}, u32[]{:S(2)}, u32[]{:S(2)}) collective-permute-start(bf16[1,2,128,256]{2,3,1,0:T(8,128)(2,1)S(1)} %copy.15), channel_id=1, source_target_pairs={{0,4},{4,8},{8,12},{12,0},{1,5},{5,9},{9,13},{13,1},{2,6},{6,10},{... | collective-permute-start | bytes 393224 | tf_op jit(solution)/shard_map/ppermute | solution.py:86
  15.0 5.9 %collective-permute-start.1 = (bf16[1,2,128,256]{2,3,1,0:T(8,128)(2,1)S(1)}, bf16[1,2,128,256]{2,3,1,0:T(8,128)(2,1)S(1)}, u32[]{:S(2)}, u32[]{:S(2)}) collective-permute-start(bf16[1,2,128,256]{2,3,1,0:T(8,128)(2,1)S(1)} %collective-permute-done), channel_id=1, source_target_pairs={{0,4},{4,8},{8,12},{12,0},{1,5},{5,9},{9,13},{13,1},{2,6},{6,10},{... | collective-permute-start | bytes 393224 | tf_op jit(solution)/shard_map/ppermute | solution.py:86
  20.9 5.9 %collective-permute-start.2 = (bf16[1,2,128,256]{2,3,1,0:T(8,128)(2,1)S(1)}, bf16[1,2,128,256]{2,3,1,0:T(8,128)(2,1)S(1)}, u32[]{:S(2)}, u32[]{:S(2)}) collective-permute-start(bf16[1,2,128,256]{2,3,1,0:T(8,128)(2,1)S(1)} %collective-permute-done.1), channel_id=1, source_target_pairs={{0,4},{4,8},{8,12},{12,0},{1,5},{5,9},{9,13},{13,1},{2,6},{6,10},{... | collective-permute-start | bytes 393224 | tf_op jit(solution)/shard_map/ppermute | solution.py:86
  28.3 30.1 %copy-start = (bf16[1,128,1024]{2,1,0:T(8,128)(2,1)S(1)}, bf16[1,128,1024]{2,1,0:T(8,128)(2,1)}, u32[]{:S(2)}) copy-start(bf16[1,128,1024]{2,1,0:T(8,128)(2,1)} %param.8) | copy-start | bytes 786436
  63.4 1.6 %collective-permute-start.3 = (bf16[1,128,1024]{2,1,0:T(8,128)(2,1)S(1)}, bf16[1,128,1024]{2,1,0:T(8,128)(2,1)S(1)}, u32[]{:S(2)}, u32[]{:S(2)}) collective-permute-start(bf16[1,128,1024]{2,1,0:T(8,128)(2,1)S(1)} %fusion.14), channel_id=1, source_target_pairs={{0,16},{16,0},{1,17},{17,1},{2,18},{18,2},{3,19},{19,3},{4,20},{20... | collective-permute-start | bytes 786440 | tf_op jit(solution)/shard_map/ppermute | solution.py:15
Sparse Core Ops, SparseCore 0:
  29.8 28.4 all-gather.1
